TPU v7x, 256 devices: a whole 4x4x8 slice. The times are simulated.
256 devices in a mesh: layer: 64 (over y, x_lo, z), feat: 4 (over x_hi, core).
Axes of the slice: x: 4 (x_hi: 2, x_lo: 2; x = x_hi * 2 + x_lo), y: 4, z: 8, core: 2. Of those that a mesh axis runs over, the one named last changes fastest.
Arguments:
- sources: bfloat16 [256, 8192], P(('layer', 'feat')), may hold values from -6 to 6
- targets: bfloat16 [256, 16384], P(('layer', 'feat')), may hold values from -16 to 16
- enc_weight: bfloat16 [8192, 32768], P(None, ('feat', 'layer')), may hold values from -0.0625 to 0.0625
- enc_bias: float32 [32768], P(('feat', 'layer')), may hold values from -3 to 3
- dec_weight: bfloat16 [32768, 16384], P('feat', 'layer'), may hold values from -0.03125 to 0.03125
- dec_bias: float32 [16384], P('layer'), may hold values from -3 to 3
Outputs:
- enc_grad: bfloat16 [8192, 32768], P(None, ('feat', 'layer'))
- dec_grad: bfloat16 [32768, 16384], P('feat', 'layer')
- mse: float32 [], replicated
All inputs are finite; a program needn't handle non-finite values.
Results may differ from a plain program's by a relative error of at most 0.011.
Values may be sent and summed in bfloat16 or wider, within the bound.
No kernel may reach another device: no remote copies, remote signals or barrier semaphores. Data moves between devices by JAX's collectives and lax.ppermute only.
A program may use at most 128 MiB of HBM per device.

v0:
```python
import math
import jax
import jax.numpy as jnp
from jax import lax
from jax.sharding import Mesh, PartitionSpec as P

LAYER = ("y", "x_lo", "z")
FEAT = ("x_hi", "core")


def spread_to(block, axes):
    n = lax.axis_size(axes)
    return lax.all_to_all(
        jnp.broadcast_to(block[None], (n, *block.shape)),
        axes,
        split_axis=0,
        concat_axis=0,
        tiled=True,
    )


def per_device(sources, targets, enc_weight, enc_bias, dec_weight, dec_bias):
    n_y, n_xl, n_z = (lax.axis_size(a) for a in LAYER)
    n_xh, n_c = (lax.axis_size(a) for a in FEAT)
    n_layer = n_y * n_xl * n_z
    rows, width = dec_weight.shape
    feats_own = enc_weight.shape[1]
    depth = sources.shape[1]
    tokens = n_layer * n_xh * n_c
    factor = 1.0 / math.sqrt(tokens)
    owned = lax.all_to_all(
        targets.reshape(n_layer, 1, width), LAYER, split_axis=0, concat_axis=0, tiled=True
    )
    wanted = lax.all_gather(owned.reshape(n_layer, width), FEAT, axis=0, tiled=True)
    wanted = (
        wanted.reshape(n_xh, n_c, n_y * n_xl, n_z, width)
        .transpose(1, 2, 0, 3, 4)
        .reshape(tokens, width)
    )
    near = spread_to(sources, "z").reshape(n_z, depth)
    half = spread_to(near, ("y", "x_lo", "x_hi")).reshape(tokens // n_c, depth)
    inputs = spread_to(half, "core").reshape(tokens, depth)
    preact = jnp.dot(inputs, enc_weight, preferred_element_type=jnp.float32) + enc_bias
    preact = preact.T
    feats = jax.nn.gelu(preact).astype(jnp.bfloat16)
    near_feats = spread_to(feats, "z").reshape(n_z * feats_own, tokens)
    all_feats = spread_to(near_feats, ("y", "x_lo")).reshape(rows, tokens)
    partial_value = lax.dot_general(
        all_feats, dec_weight, (((0,), (0,)), ((), ())), preferred_element_type=jnp.float32
    ).astype(jnp.bfloat16)
    parts = lax.all_gather(partial_value, FEAT, axis=0)
    outputs = jnp.sum(parts.astype(jnp.float32), axis=0) + dec_bias
    misfit = outputs - wanted.astype(jnp.float32)
    errors = (misfit * factor).astype(jnp.bfloat16)
    own_sq = jnp.broadcast_to(jnp.sum(misfit * misfit), (n_layer, 1, 128))
    every_sq = lax.all_to_all(own_sq, LAYER, split_axis=0, concat_axis=0, tiled=True)
    mse = jnp.sum(every_sq[:, 0, 0]) / (tokens * n_layer * width)
    grads = lax.dot_general(
        dec_weight, errors, (((1,), (1,)), ((), ())), preferred_element_type=jnp.float32
    ).astype(jnp.bfloat16)
    far = lax.all_to_all(
        grads.reshape(n_y * n_xl, n_z * feats_own, tokens),
        ("y", "x_lo"),
        split_axis=0,
        concat_axis=0,
        tiled=True,
    )
    far = jnp.sum(far.astype(jnp.float32), axis=0).astype(jnp.bfloat16)
    close = lax.all_to_all(
        far.reshape(n_z, feats_own, tokens), "z", split_axis=0, concat_axis=0, tiled=True
    )
    feat_grad = jnp.sum(close.astype(jnp.float32), axis=0)
    dec_grad = jnp.dot(all_feats, errors, preferred_element_type=jnp.float32).astype(jnp.bfloat16)
    _, pullback = jax.vjp(jax.nn.gelu, preact)
    pre_grad = pullback(feat_grad)[0].astype(jnp.bfloat16)
    enc_grad = lax.dot_general(
        inputs, pre_grad, (((0,), (1,)), ((), ())), preferred_element_type=jnp.float32
    ).astype(jnp.bfloat16)
    return (enc_grad, dec_grad, mse)


def solution(mesh):
    n_layer, n_feat = mesh.devices.shape
    n_x_lo, n_z = (2, 8)
    torus = Mesh(
        mesh.devices.reshape(n_layer // (n_x_lo * n_z), n_x_lo, n_z, n_feat // 2, 2),
        (*LAYER, *FEAT),
    )
    return jax.shard_map(
        per_device,
        mesh=torus,
        in_specs=(
            P((*LAYER, *FEAT), None),
            P((*LAYER, *FEAT), None),
            P(None, (*FEAT, *LAYER)),
            P((*FEAT, *LAYER)),
            P(FEAT, LAYER),
            P(LAYER),
        ),
        out_specs=(P(None, (*FEAT, *LAYER)), P(FEAT, LAYER), P()),
        check_vma=False,
    )
```

profile of v0, /device:TPU:1, one launch (start us, length us, event | category | flops | bytes accessed | tf_op | source)
XLA Modules:
  0.0 274.8 jit_solution(3152163767902077613)
XLA Ops:
  0.6 0.0 copy-start
  0.6 1.0 reduce.3
  1.6 0.0 copy-start.2
  1.7 0.1 broadcast_in_dim.41
  1.8 0.5 broadcast.54
  2.3 1.4 reduce.4
  3.7 0.1 reshape.69
  3.8 16.6 %all_to_all.45 = bf16[8,2,4096]{2,1,0:T(2,128)(2,1)S(1)} all-to-all(bf16[8,2,4096]{2,1,0:T(2,128)(2,1)S(1)} %reshape.69), channel_id=1, replica_groups=mesh['y'=4,'x_lo'=2,'z'=8,'x_hi'=2,'core'=2] {'z'}, dimensions={0} | all-to-all | bytes 262144 | tf_op jit(solution)/shard_map/all_to_all | solution.py:13
  20.4 0.1 reshape.70
  20.5 0.2 copy.73
  20.6 1.5 broadcast_in_dim.43
  22.2 6.8 %all-to-all-start.1 = ((bf16[16,8,8192]{2,1,0:T(8,128)(2,1)}), bf16[16,8,8192]{2,1,0:T(8,128)(2,1)}, u32[]{:S(2)}, u32[]{:S(2)}) async-start(bf16[16,8,8192]{2,1,0:T(8,128)(2,1)} %broadcast_in_dim.43), calls=%async_computation.1 | async-start | bytes 4194304 | tf_op jit(solution)/shard_map/all_to_all | solution.py:13
  29.0 0.8 reduce.5
  29.8 0.6 reshape.71
  30.5 23.9 %all-to-all-done.1 = bf16[16,8,8192]{2,1,0:T(8,128)(2,1)} async-done(((bf16[16,8,8192]{2,1,0:T(8,128)(2,1)}), bf16[16,8,8192]{2,1,0:T(8,128)(2,1)}, u32[]{:S(2)}, u32[]{:S(2)}) %all-to-all-start.1) | async-done | bytes 2097184 | tf_op jit(solution)/shard_map/all_to_all | solution.py:13
  54.3 2.1 broadcast_in_dim.45
  56.4 0.0 copy-start.4
  56.4 10.4 %all_to_all.46 = bf16[2,128,8192]{2,1,0:T(8,128)(2,1)} all-to-all(bf16[2,128,8192]{2,1,0:T(8,128)(2,1)S(1)} %broadcast_in_dim.45), channel_id=1, replica_groups=mesh['y'=4,'x_lo'=2,'z'=8,'x_hi'=2,'core'=2] {'core'}, dimensions={0} | all-to-all | bytes 8388608 | tf_op jit(solution)/shard_map/all_to_all | solution.py:13
  66.8 5.7 %all-to-all-start.5 = ((bf16[64,2,128]{2,1,0:T(2,128)(2,1)}), bf16[64,2,128]{2,1,0:T(2,128)(2,1)S(1)}, u32[]{:S(2)}, u32[]{:S(2)}) async-start(bf16[64,2,128]{2,1,0:T(2,128)(2,1)} %reshape.71), calls=%async_computation.5 | async-start | bytes 65536 | tf_op jit(solution)/shard_map/all_to_all | solution.py:31
  72.6 3.7 %multiply_convert_fusion.1 = (bf16[128,256]{1,0:T(8,128)(2,1)S(1)}, f32[128,256]{1,0:T(8,128)S(1)}) fusion(f32[128]{0:T(128)S(1)} %copy-done.4, bf16[8192,128]{1,0:T(8,128)(2,1)S(1)} %copy-done, bf16[256,8192]{1,0:T(8,128)(2,1)} %bitcast.47), kind=kOutput, calls=%fused_computation.28 | convolution fusion | flops 537198592 | bytes 6488576 | tf_op jit(solution)/shard_map/dot_general | solution.py:43
  76.3 5.5 %all-to-all-done.5 = bf16[64,2,128]{2,1,0:T(2,128)(2,1)S(1)} async-done(((bf16[64,2,128]{2,1,0:T(2,128)(2,1)}), bf16[64,2,128]{2,1,0:T(2,128)(2,1)S(1)}, u32[]{:S(2)}, u32[]{:S(2)}) %all-to-all-start.5) | async-done | bytes 32800 | tf_op jit(solution)/shard_map/all_to_all | solution.py:31
  81.8 17.4 %all_to_all.47 = bf16[8,128,256]{2,1,0:T(8,128)(2,1)S(1)} all-to-all(bf16[8,128,256]{2,1,0:T(8,128)(2,1)S(1)} %broadcast_in_dim.46), channel_id=1, replica_groups=mesh['y'=4,'x_lo'=2,'z'=8,'x_hi'=2,'core'=2] {'z'}, dimensions={0} | all-to-all | bytes 1048576 | tf_op jit(solution)/shard_map/all_to_all | solution.py:13
  99.3 2.3 broadcast_in_dim.48
  101.6 4.5 %all-to-all-start.4 = ((bf16[8,1024,256]{2,1,0:T(8,128)(2,1)}), bf16[8,1024,256]{2,1,0:T(8,128)(2,1)}, u32[]{:S(2)}, u32[]{:S(2)}) async-start(bf16[8,1024,256]{2,1,0:T(8,128)(2,1)} %broadcast_in_dim.48), calls=%async_computation.4 | async-start | bytes 8388608 | tf_op jit(solution)/shard_map/all_to_all | solution.py:13
  106.2 51.4 %all-gather.1 = bf16[256,1,256]{2,0,1:T(8,128)(2,1)S(1)} all-gather(bf16[64,1,256]{2,0,1:T(8,128)(2,1)S(1)} %copy.44), channel_id=3, replica_groups=mesh['y'=4,'x_lo'=2,'z'=8,'x_hi'=2,'core'=2] {'x_hi','core'}, dimensions={0}, use_global_device_ids=true | all-gather | bytes 163840 | tf_op jit(solution)/shard_map/all_gather | solution.py:34
  157.6 0.0 copy-start.3
  157.7 0.0 copy-start.1
  157.7 4.9 %convolution_convert_fusion.3 = bf16[256,256]{1,0:T(8,128)(2,1)S(1)} fusion(bf16[8192,256]{1,0:T(8,128)(2,1)} %bitcast.3, bf16[8192,256]{1,0:T(8,128)(2,1)} %param.10), kind=kOutput, calls=%fused_computation.5 | convolution fusion | flops 1073807360 | bytes 8519680 | tf_op jit(solution)/shard_map/dot_general | solution.py:48
  162.6 8.8 %all-gather = bf16[1024,256]{1,0:T(8,128)(2,1)S(1)} all-gather(bf16[256,256]{1,0:T(8,128)(2,1)S(1)} %convolution_convert_fusion.3), channel_id=2, replica_groups=mesh['y'=4,'x_lo'=2,'z'=8,'x_hi'=2,'core'=2] {'x_hi','core'}, dimensions={0}, use_global_device_ids=true | all-gather | bytes 655360 | tf_op jit(solution)/shard_map/all_gather | solution.py:51
  171.4 0.1 convert_reduce_fusion
  171.5 1.3 convolution_convert_fusion.1
  172.8 2.5 copy.72
  175.2 4.9 %all-to-all-start.6 = ((bf16[8,1024,256]{1,2,0:T(8,128)(2,1)}), bf16[8,1024,256]{1,2,0:T(8,128)(2,1)}, u32[]{:S(2)}, u32[]{:S(2)}) async-start(bf16[8,1024,256]{1,2,0:T(8,128)(2,1)} %bitcast.49), calls=%async_computation.6 | async-start | bytes 8388608 | tf_op jit(solution)/shard_map/all_to_all | solution.py:61
  180.2 0.7 multiply_reduce_fusion
  180.8 48.5 %all-to-all-done.6 = bf16[8,1024,256]{1,2,0:T(8,128)(2,1)} async-done(((bf16[8,1024,256]{1,2,0:T(8,128)(2,1)}), bf16[8,1024,256]{1,2,0:T(8,128)(2,1)}, u32[]{:S(2)}, u32[]{:S(2)}) %all-to-all-start.6) | async-done | bytes 4194336 | tf_op jit(solution)/shard_map/all_to_all | solution.py:61
  229.4 1.3 broadcast_in_dim.49
  230.7 5.8 %all-to-all-start.8 = ((f32[64,1,128]{2,1,0:T(1,128)}), f32[64,1,128]{2,1,0:T(1,128)S(1)}, u32[]{:S(2)}, u32[]{:S(2)}) async-start(f32[64,1,128]{2,1,0:T(1,128)} %broadcast_in_dim.49), calls=%async_computation.8 | async-start | bytes 65536 | tf_op jit(solution)/shard_map/all_to_all | solution.py:56
  236.5 3.1 %reduce_sum.51 = bf16[1024,256]{0,1:T(8,128)(2,1)S(1)} reduce(bf16[8,1024,256]{1,2,0:T(8,128)(2,1)} %all-to-all-done.6, bf16[]{:T(256)} %constant.17.clone.1), dimensions={0}, to_apply=%region_1.0 | reduce | flops 1835008 | bytes 4718594 | tf_op jit(solution)/shard_map/reduce_sum | solution.py:68
  239.6 0.9 copy_bitcast_fusion.1
  240.5 5.2 %all-to-all-done.8 = f32[64,1,128]{2,1,0:T(1,128)S(1)} async-done(((f32[64,1,128]{2,1,0:T(1,128)}), f32[64,1,128]{2,1,0:T(1,128)S(1)}, u32[]{:S(2)}, u32[]{:S(2)}) %all-to-all-start.8) | async-done | bytes 32800 | tf_op jit(solution)/shard_map/all_to_all | solution.py:56
  245.7 3.7 %all-to-all-start.7 = ((bf16[8,128,256]{1,2,0:T(8,128)(2,1)}), bf16[8,128,256]{1,2,0:T(8,128)(2,1)S(1)}, u32[]{:S(2)}, u32[]{:S(2)}) async-start(bf16[8,128,256]{1,2,0:T(8,128)(2,1)} %copy_bitcast_fusion.1), calls=%async_computation.7 | async-start | bytes 1048576 | tf_op jit(solution)/shard_map/all_to_all | solution.py:69
  249.4 5.5 %convolution_convert_fusion = bf16[8192,256]{1,0:T(8,128)(2,1)} fusion(bf16[8192,256]{1,0:T(8,128)(2,1)} %bitcast.3, bf16[256,256]{1,0:T(8,128)(2,1)S(1)} %bitcast.56), kind=kOutput, calls=%fused_computation | convolution fusion | flops 1075838976 | bytes 8519680 | tf_op jit(solution)/shard_map/dot_general | solution.py:73
  254.9 0.7 slice_reduce_fusion
  256.2 9.0 %all-to-all-done.7 = bf16[8,128,256]{1,2,0:T(8,128)(2,1)S(1)} async-done(((bf16[8,128,256]{1,2,0:T(8,128)(2,1)}), bf16[8,128,256]{1,2,0:T(8,128)(2,1)S(1)}, u32[]{:S(2)}, u32[]{:S(2)}) %all-to-all-start.7) | async-done | bytes 524320 | tf_op jit(solution)/shard_map/all_to_all | solution.py:69
  265.1 0.1 convert_reduce_fusion.1
  265.2 0.1 copy.50
  265.3 4.3 %fusion = bf16[8192,128]{0,1:T(8,128)(2,1)} fusion(bf16[256,8192]{1,0:T(8,128)(2,1)} %bitcast.48, f32[128,256]{1,0:T(8,128)S(1)} %get-tuple-element.27, f32[128,256]{1,0:T(8,128)S(1)} %copy.50), kind=kOutput, calls=%fused_computation.3 | convolution fusion | flops 538574848 | bytes 6553600 | tf_op jit(solution)/shard_map/dot_general | solution.py:76
  269.6 4.1 %copy.55 = bf16[8192,128]{1,0:T(8,128)(2,1)} copy(bf16[8192,128]{0,1:T(8,128)(2,1)} %fusion) | data formatting | bytes 4194304
  (13 shorter events, 0.2 us)
Async XLA Ops:
  0.6 71.9 %copy-start = (bf16[8192,128]{1,0:T(8,128)(2,1)S(1)}, bf16[8192,128]{1,0:T(8,128)(2,1)}, u32[]{:S(2)}) copy-start(bf16[8192,128]{1,0:T(8,128)(2,1)} %param.8) | copy-start | bytes 6291460
  1.6 27.3 %copy-start.2 = (bf16[1,16384]{1,0:T(2,128)(2,1)S(1)}, bf16[1,16384]{1,0:T(2,128)(2,1)}, u32[]{:S(2)}) copy-start(bf16[1,16384]{1,0:T(2,128)(2,1)} %param.7) | copy-start | bytes 98308
  22.2 32.2 %all-to-all-start.1 = ((bf16[16,8,8192]{2,1,0:T(8,128)(2,1)}), bf16[16,8,8192]{2,1,0:T(8,128)(2,1)}, u32[]{:S(2)}, u32[]{:S(2)}) async-start(bf16[16,8,8192]{2,1,0:T(8,128)(2,1)} %broadcast_in_dim.43), calls=%async_computation.1 | async-start | bytes 4194304 | tf_op jit(solution)/shard_map/all_to_all | solution.py:13
  56.4 16.2 %copy-start.4 = (f32[128]{0:T(128)S(1)}, f32[128]{0:T(128)}, u32[]{:S(2)}) copy-start(f32[128]{0:T(128)} %param.9) | copy-start | bytes 1540
  66.8 15.0 %all-to-all-start.5 = ((bf16[64,2,128]{2,1,0:T(2,128)(2,1)}), bf16[64,2,128]{2,1,0:T(2,128)(2,1)S(1)}, u32[]{:S(2)}, u32[]{:S(2)}) async-start(bf16[64,2,128]{2,1,0:T(2,128)(2,1)} %reshape.71), calls=%async_computation.5 | async-start | bytes 65536 | tf_op jit(solution)/shard_map/all_to_all | solution.py:31
  101.6 56.1 %all-to-all-start.4 = ((bf16[8,1024,256]{2,1,0:T(8,128)(2,1)}), bf16[8,1024,256]{2,1,0:T(8,128)(2,1)}, u32[]{:S(2)}, u32[]{:S(2)}) async-start(bf16[8,1024,256]{2,1,0:T(8,128)(2,1)} %broadcast_in_dim.48), calls=%async_computation.4 | async-start | bytes 8388608 | tf_op jit(solution)/shard_map/all_to_all | solution.py:13
  157.6 13.8 %copy-start.3 = (f32[256]{0:T(256)S(1)}, f32[256]{0:T(256)}, u32[]{:S(2)}) copy-start(f32[256]{0:T(256)} %param.11) | copy-start | bytes 3076
  157.7 13.8 %copy-start.1 = (bf16[8192,256]{1,0:T(8,128)(2,1)S(1)}, bf16[8192,256]{1,0:T(8,128)(2,1)}, u32[]{:S(2)}) copy-start(bf16[8192,256]{1,0:T(8,128)(2,1)} %param.10) | copy-start | bytes 12582916
  175.2 54.1 %all-to-all-start.6 = ((bf16[8,1024,256]{1,2,0:T(8,128)(2,1)}), bf16[8,1024,256]{1,2,0:T(8,128)(2,1)}, u32[]{:S(2)}, u32[]{:S(2)}) async-start(bf16[8,1024,256]{1,2,0:T(8,128)(2,1)} %bitcast.49), calls=%async_computation.6 | async-start | bytes 8388608 | tf_op jit(solution)/shard_map/all_to_all | solution.py:61
  230.7 15.0 %all-to-all-start.8 = ((f32[64,1,128]{2,1,0:T(1,128)}), f32[64,1,128]{2,1,0:T(1,128)S(1)}, u32[]{:S(2)}, u32[]{:S(2)}) async-start(f32[64,1,128]{2,1,0:T(1,128)} %broadcast_in_dim.49), calls=%async_computation.8 | async-start | bytes 65536 | tf_op jit(solution)/shard_map/all_to_all | solution.py:56
  245.7 19.4 %all-to-all-start.7 = ((bf16[8,128,256]{1,2,0:T(8,128)(2,1)}), bf16[8,128,256]{1,2,0:T(8,128)(2,1)S(1)}, u32[]{:S(2)}, u32[]{:S(2)}) async-start(bf16[8,128,256]{1,2,0:T(8,128)(2,1)} %copy_bitcast_fusion.1), calls=%async_computation.7 | async-start | bytes 1048576 | tf_op jit(solution)/shard_map/all_to_all | solution.py:69
where the time goes:
time: 276 us; the launch traced here: 275 us
  blocking collectives  105 us (38%)
  waiting for transfers between devices  92.1 us (33%)
  starting transfers between devices  31.5 us (11%)
  matrix products  19.7 us (7%)
  local copies, waits for them, and re-layouts  16.4 us (6%)
  other arithmetic  7.86 us (3%)
    all_gather x1, blocking collectives, per_device(): lax.all_gather(owned.reshape(n_layer, width), FEAT, axis=0, tiled=True)  51.4 us
    all_to_all x1, waiting for transfers between devices, per_device(): lax.all_to_all(grads.reshape(n_y * n_xl, n_z * feats_own, tokens), ('y',...  48.5 us
    all_to_all x3, blocking collectives, spread_to(): lax.all_to_all(jnp.broadcast_to(block[None], (n, *block.shape)), axes, sp...  44.4 us
    all_to_all x2, waiting for transfers between devices, spread_to(): lax.all_to_all(jnp.broadcast_to(block[None], (n, *block.shape)), axes, sp...  23.9 us
    all_to_all x2, starting transfers between devices, spread_to(): lax.all_to_all(jnp.broadcast_to(block[None], (n, *block.shape)), axes, sp...  11.4 us
    all_to_all x1, waiting for transfers between devices, per_device(): lax.all_to_all(far.reshape(n_z, feats_own, tokens), 'z', split_axis=0, co...  8.96 us
    all_gather x1, blocking collectives, per_device(): parts = lax.all_gather(partial_value, FEAT, axis=0)  8.78 us
    broadcast_in_dim x6, local copies, waits for them, and re-layouts, spread_to(): jnp.broadcast_to(block[None], (n, *block.shape))  6.54 us
  transfers between devices with their start and end apart: 6, of which 5 were waited for; matrix products, arithmetic and copies ran while one was open for 6% of the time, Pallas kernels for 0%

commit v1 on v0

--- a/solution.py
+++ b/solution.py
@@ -1,3 +1,4 @@
+import functools
 import math
 import jax
 import jax.numpy as jnp
@@ -6,6 +7,14 @@
 
 LAYER = ("y", "x_lo", "z")
 FEAT = ("x_hi", "core")
+
+
+def _treat_sheets(vec, peer_axis):
+    placed = lax.all_to_all(jnp.stack([vec] * lax.psum(1, peer_axis), axis=0), peer_axis, 0, 0)
+    return jnp.concatenate(placed, 0)
+
+
+heaps_number = functools.partial(_treat_sheets, peer_axis=FEAT)
 
 
 def spread_to(block, axes):
@@ -31,7 +40,7 @@
     owned = lax.all_to_all(
         targets.reshape(n_layer, 1, width), LAYER, split_axis=0, concat_axis=0, tiled=True
     )
-    wanted = lax.all_gather(owned.reshape(n_layer, width), FEAT, axis=0, tiled=True)
+    wanted = heaps_number(owned.reshape(n_layer, width))
     wanted = (
         wanted.reshape(n_xh, n_c, n_y * n_xl, n_z, width)
         .transpose(1, 2, 0, 3, 4)

time: 276 us -> 285 us (1.033)
  blocking collectives: 105 us -> 42.8 us
  waiting for transfers between devices: 92.1 us -> 149 us
  starting transfers between devices: 31.5 us -> 43.4 us
    all_to_all x2 -> x3, waiting for transfers between devices: 23.9 us -> 76.5 us  [spread_to(): lax.all_to_all(jnp.broadcast_to(block[None], (n, *block.shape)), axes, sp...]
    all_gather x1 -> x0, blocking collectives: 51.4 us -> none  [per_device(): lax.all_gather(owned.reshape(n_layer, width), FEAT, axis=0, tiled=True)]
    all_to_all x3 -> x2, blocking collectives: 44.4 us -> 30.1 us  [spread_to(): lax.all_to_all(jnp.broadcast_to(block[None], (n, *block.shape)), axes, sp...]
    all_to_all x2 -> x3, starting transfers between devices: 11.4 us -> 18.1 us  [spread_to(): lax.all_to_all(jnp.broadcast_to(block[None], (n, *block.shape)), axes, sp...]
    all_to_all x0 -> x1, starting transfers between devices: none -> 5.53 us  [_treat_sheets(): lax.all_to_all(jnp.stack([vec] * lax.psum(1, peer_axis), axis=0), peer_ax...]
    all_gather x1, blocking collectives: 8.78 us -> 12.7 us  [per_device(): parts = lax.all_gather(partial_value, FEAT, axis=0)]
    all_to_all x1, waiting for transfers between devices: 5.48 us -> 8.92 us  [per_device(): lax.all_to_all(targets.reshape(n_layer, 1, width), LAYER, split_axis=0, c...]
    unnamed x16 -> x15, local copies, waits for them, and re-layouts: 5.09 us -> 5.75 us
  transfers between devices with their start and end apart: 6 -> 8, of which waited for: 5 -> 8; matrix products, arithmetic and copies ran while one was open for 6% -> 6% of each run, Pallas kernels for 0% -> 0%
where the time goes in v1:
time: 285 us; the launch traced here: 284 us
  waiting for transfers between devices  149 us (52%)
  starting transfers between devices  43.4 us (15%)
  blocking collectives  42.8 us (15%)
  matrix products  19.7 us (7%)
  local copies, waits for them, and re-layouts  17.7 us (6%)
  other arithmetic  8.7 us (3%)
    all_to_all x3, waiting for transfers between devices, spread_to(): lax.all_to_all(jnp.broadcast_to(block[None], (n, *block.shape)), axes, sp...  76.5 us
    all_to_all x1, waiting for transfers between devices, per_device(): lax.all_to_all(grads.reshape(n_y * n_xl, n_z * feats_own, tokens), ('y',...  48.7 us
    all_to_all x2, blocking collectives, spread_to(): lax.all_to_all(jnp.broadcast_to(block[None], (n, *block.shape)), axes, sp...  30.1 us
    all_to_all x3, starting transfers between devices, spread_to(): lax.all_to_all(jnp.broadcast_to(block[None], (n, *block.shape)), axes, sp...  18.1 us
    all_gather x1, blocking collectives, per_device(): parts = lax.all_gather(partial_value, FEAT, axis=0)  12.7 us
    all_to_all x1, waiting for transfers between devices, per_device(): lax.all_to_all(targets.reshape(n_layer, 1, width), LAYER, split_axis=0, c...  8.92 us
    all_to_all x1, waiting for transfers between devices, per_device(): lax.all_to_all(far.reshape(n_z, feats_own, tokens), 'z', split_axis=0, co...  8.67 us
    all_to_all x1, starting transfers between devices, per_device(): lax.all_to_all(targets.reshape(n_layer, 1, width), LAYER, split_axis=0, c...  6.85 us
  transfers between devices with their start and end apart: 8, of which 8 were waited for; matrix products, arithmetic and copies ran while one was open for 6% of the time, Pallas kernels for 0%

profile of v1, /device:TPU:1, one launch (start us, length us, event | category | flops | bytes accessed | tf_op | source)
XLA Modules:
  0.0 284.2 jit_solution(16637828269328250067)
XLA Ops:
  0.6 0.0 copy-start
  0.6 1.0 reduce.3
  1.6 0.1 broadcast_in_dim.41
  1.8 0.5 broadcast.55
  2.3 1.4 reduce.4
  3.7 0.7 reshape.61
  4.4 9.0 %all-to-all-start = ((bf16[8,2,4096]{2,1,0:T(2,128)(2,1)}), bf16[8,2,4096]{2,1,0:T(2,128)(2,1)S(1)}, u32[]{:S(2)}, u32[]{:S(2)}) async-start(bf16[8,2,4096]{2,1,0:T(2,128)(2,1)} %reshape.61), calls=%async_computation | async-start | bytes 262144 | tf_op jit(solution)/shard_map/all_to_all | solution.py:22
  13.5 1.7 reduce.5
  15.1 0.6 reshape.63
  15.7 5.5 %all-to-all-done = bf16[8,2,4096]{2,1,0:T(2,128)(2,1)S(1)} async-done(((bf16[8,2,4096]{2,1,0:T(2,128)(2,1)}), bf16[8,2,4096]{2,1,0:T(2,128)(2,1)S(1)}, u32[]{:S(2)}, u32[]{:S(2)}) %all-to-all-start) | async-done | bytes 131104 | tf_op jit(solution)/shard_map/all_to_all | solution.py:22
  21.2 6.9 %all-to-all-start.5 = ((bf16[64,2,128]{2,1,0:T(2,128)(2,1)}), bf16[64,2,128]{2,1,0:T(2,128)(2,1)S(1)}, u32[]{:S(2)}, u32[]{:S(2)}) async-start(bf16[64,2,128]{2,1,0:T(2,128)(2,1)} %reshape.63), calls=%async_computation.5 | async-start | bytes 65536 | tf_op jit(solution)/shard_map/all_to_all | solution.py:40
  28.1 0.1 reshape.62
  28.2 0.2 copy.77
  28.4 8.9 %all-to-all-done.5 = bf16[64,2,128]{2,1,0:T(2,128)(2,1)S(1)} async-done(((bf16[64,2,128]{2,1,0:T(2,128)(2,1)}), bf16[64,2,128]{2,1,0:T(2,128)(2,1)S(1)}, u32[]{:S(2)}, u32[]{:S(2)}) %all-to-all-start.5) | async-done | bytes 32800 | tf_op jit(solution)/shard_map/all_to_all | solution.py:40
  37.3 1.5 broadcast_in_dim.43
  38.8 4.6 %all-to-all-start.1 = ((bf16[16,8,8192]{2,1,0:T(8,128)(2,1)}), bf16[16,8,8192]{2,1,0:T(8,128)(2,1)}, u32[]{:S(2)}, u32[]{:S(2)}) async-start(bf16[16,8,8192]{2,1,0:T(8,128)(2,1)} %broadcast_in_dim.43), calls=%async_computation.1 | async-start | bytes 4194304 | tf_op jit(solution)/shard_map/all_to_all | solution.py:22
  43.4 24.0 %all-to-all-done.1 = bf16[16,8,8192]{2,1,0:T(8,128)(2,1)} async-done(((bf16[16,8,8192]{2,1,0:T(8,128)(2,1)}), bf16[16,8,8192]{2,1,0:T(8,128)(2,1)}, u32[]{:S(2)}, u32[]{:S(2)}) %all-to-all-start.1) | async-done | bytes 2097184 | tf_op jit(solution)/shard_map/all_to_all | solution.py:22
  67.4 2.1 broadcast_in_dim.45
  69.5 11.7 %all_to_all.50 = bf16[2,128,8192]{2,1,0:T(8,128)(2,1)} all-to-all(bf16[2,128,8192]{2,1,0:T(8,128)(2,1)S(1)} %broadcast_in_dim.45), channel_id=1, replica_groups=mesh['y'=4,'x_lo'=2,'z'=8,'x_hi'=2,'core'=2] {'core'}, dimensions={0} | all-to-all | bytes 8388608 | tf_op jit(solution)/shard_map/all_to_all | solution.py:22
  81.2 0.7 stack.3
  81.9 5.5 %all-to-all-start.6 = ((bf16[4,64,256]{2,1,0:T(8,128)(2,1)}), bf16[4,64,256]{2,1,0:T(8,128)(2,1)S(1)}, u32[]{:S(2)}, u32[]{:S(2)}) async-start(bf16[4,64,256]{2,1,0:T(8,128)(2,1)} %stack.3), calls=%async_computation.6 | async-start | bytes 262144 | tf_op jit(solution)/shard_map/all_to_all | solution.py:13
  87.4 3.7 %multiply_convert_fusion.1 = (bf16[128,256]{1,0:T(8,128)(2,1)S(1)}, f32[128,256]{1,0:T(8,128)S(1)}) fusion(f32[128]{0:T(128)S(1)} %copy-done.3, bf16[8192,128]{1,0:T(8,128)(2,1)S(1)} %copy-done, bf16[256,8192]{1,0:T(8,128)(2,1)} %bitcast.50), kind=kOutput, calls=%fused_computation.28 | convolution fusion | flops 537198592 | bytes 6488576 | tf_op jit(solution)/shard_map/dot_general | solution.py:52
  91.2 1.3 all-to-all-done.6
  92.5 18.3 %all_to_all.51 = bf16[8,128,256]{2,1,0:T(8,128)(2,1)S(1)} all-to-all(bf16[8,128,256]{2,1,0:T(8,128)(2,1)S(1)} %broadcast_in_dim.46), channel_id=1, replica_groups=mesh['y'=4,'x_lo'=2,'z'=8,'x_hi'=2,'core'=2] {'z'}, dimensions={0} | all-to-all | bytes 1048576 | tf_op jit(solution)/shard_map/all_to_all | solution.py:22
  110.9 2.3 broadcast_in_dim.48
  113.2 4.5 %all-to-all-start.4 = ((bf16[8,1024,256]{2,1,0:T(8,128)(2,1)}), bf16[8,1024,256]{2,1,0:T(8,128)(2,1)}, u32[]{:S(2)}, u32[]{:S(2)}) async-start(bf16[8,1024,256]{2,1,0:T(8,128)(2,1)} %broadcast_in_dim.48), calls=%async_computation.4 | async-start | bytes 8388608 | tf_op jit(solution)/shard_map/all_to_all | solution.py:22
  117.8 47.0 %all-to-all-done.4 = bf16[8,1024,256]{2,1,0:T(8,128)(2,1)} async-done(((bf16[8,1024,256]{2,1,0:T(8,128)(2,1)}), bf16[8,1024,256]{2,1,0:T(8,128)(2,1)}, u32[]{:S(2)}, u32[]{:S(2)}) %all-to-all-start.4) | async-done | bytes 4194336 | tf_op jit(solution)/shard_map/all_to_all | solution.py:22
  164.8 4.9 %convolution_convert_fusion.3 = bf16[256,256]{1,0:T(8,128)(2,1)S(1)} fusion(bf16[8192,256]{1,0:T(8,128)(2,1)} %bitcast.3, bf16[8192,256]{1,0:T(8,128)(2,1)} %param.10), kind=kOutput, calls=%fused_computation.5 | convolution fusion | flops 1073807360 | bytes 8519680 | tf_op jit(solution)/shard_map/dot_general | solution.py:57
  169.7 12.7 %all-gather = bf16[1024,256]{1,0:T(8,128)(2,1)S(1)} all-gather(bf16[256,256]{1,0:T(8,128)(2,1)S(1)} %convolution_convert_fusion.3), channel_id=2, replica_groups=mesh['y'=4,'x_lo'=2,'z'=8,'x_hi'=2,'core'=2] {'x_hi','core'}, dimensions={0}, use_global_device_ids=true | all-gather | bytes 655360 | tf_op jit(solution)/shard_map/all_gather | solution.py:60
  182.4 0.1 convert_reduce_fusion
  182.5 1.3 convolution_convert_fusion.1
  183.8 2.5 copy.76
  186.3 4.6 %all-to-all-start.7 = ((bf16[8,1024,256]{1,2,0:T(8,128)(2,1)}), bf16[8,1024,256]{1,2,0:T(8,128)(2,1)}, u32[]{:S(2)}, u32[]{:S(2)}) async-start(bf16[8,1024,256]{1,2,0:T(8,128)(2,1)} %bitcast.52), calls=%async_computation.7 | async-start | bytes 8388608 | tf_op jit(solution)/shard_map/all_to_all | solution.py:70
  190.9 0.7 multiply_reduce_fusion
  191.5 48.7 %all-to-all-done.7 = bf16[8,1024,256]{1,2,0:T(8,128)(2,1)} async-done(((bf16[8,1024,256]{1,2,0:T(8,128)(2,1)}), bf16[8,1024,256]{1,2,0:T(8,128)(2,1)}, u32[]{:S(2)}, u32[]{:S(2)}) %all-to-all-start.7) | async-done | bytes 4194336 | tf_op jit(solution)/shard_map/all_to_all | solution.py:70
  240.3 1.3 broadcast_in_dim.49
  241.6 4.6 %all-to-all-start.9 = ((f32[64,1,128]{2,1,0:T(1,128)}), f32[64,1,128]{2,1,0:T(1,128)S(1)}, u32[]{:S(2)}, u32[]{:S(2)}) async-start(f32[64,1,128]{2,1,0:T(1,128)} %broadcast_in_dim.49), calls=%async_computation.9 | async-start | bytes 65536 | tf_op jit(solution)/shard_map/all_to_all | solution.py:65
  246.2 3.1 %reduce_sum.51 = bf16[1024,256]{0,1:T(8,128)(2,1)S(1)} reduce(bf16[8,1024,256]{1,2,0:T(8,128)(2,1)} %all-to-all-done.7, bf16[]{:T(256)} %constant.17.clone.1), dimensions={0}, to_apply=%region_1.0 | reduce | flops 1835008 | bytes 4718594 | tf_op jit(solution)/shard_map/reduce_sum | solution.py:77
  249.3 0.9 copy_bitcast_fusion.1
  250.1 5.2 %all-to-all-done.9 = f32[64,1,128]{2,1,0:T(1,128)S(1)} async-done(((f32[64,1,128]{2,1,0:T(1,128)}), f32[64,1,128]{2,1,0:T(1,128)S(1)}, u32[]{:S(2)}, u32[]{:S(2)}) %all-to-all-start.9) | async-done | bytes 32800 | tf_op jit(solution)/shard_map/all_to_all | solution.py:65
  255.4 3.7 %all-to-all-start.8 = ((bf16[8,128,256]{1,2,0:T(8,128)(2,1)}), bf16[8,128,256]{1,2,0:T(8,128)(2,1)S(1)}, u32[]{:S(2)}, u32[]{:S(2)}) async-start(bf16[8,128,256]{1,2,0:T(8,128)(2,1)} %copy_bitcast_fusion.1), calls=%async_computation.8 | async-start | bytes 1048576 | tf_op jit(solution)/shard_map/all_to_all | solution.py:78
  259.1 5.5 %convolution_convert_fusion = bf16[8192,256]{1,0:T(8,128)(2,1)} fusion(bf16[8192,256]{1,0:T(8,128)(2,1)} %bitcast.3, bf16[256,256]{1,0:T(8,128)(2,1)S(1)} %bitcast.59), kind=kOutput, calls=%fused_computation | convolution fusion | flops 1075838976 | bytes 8519680 | tf_op jit(solution)/shard_map/dot_general | solution.py:82
  264.5 0.7 slice_reduce_fusion
  265.8 8.7 %all-to-all-done.8 = bf16[8,128,256]{1,2,0:T(8,128)(2,1)S(1)} async-done(((bf16[8,128,256]{1,2,0:T(8,128)(2,1)}), bf16[8,128,256]{1,2,0:T(8,128)(2,1)S(1)}, u32[]{:S(2)}, u32[]{:S(2)}) %all-to-all-start.8) | async-done | bytes 524320 | tf_op jit(solution)/shard_map/all_to_all | solution.py:78
  274.5 0.1 convert_reduce_fusion.1
  274.6 0.1 copy.52
  274.7 4.3 %fusion = bf16[8192,128]{0,1:T(8,128)(2,1)} fusion(bf16[256,8192]{1,0:T(8,128)(2,1)} %bitcast.51, f32[128,256]{1,0:T(8,128)S(1)} %get-tuple-element.30, f32[128,256]{1,0:T(8,128)S(1)} %copy.52), kind=kOutput, calls=%fused_computation.3 | convolution fusion | flops 538574848 | bytes 6553600 | tf_op jit(solution)/shard_map/dot_general | solution.py:85
  279.0 4.1 %copy.57 = bf16[8192,128]{1,0:T(8,128)(2,1)} copy(bf16[8192,128]{0,1:T(8,128)(2,1)} %fusion) | data formatting | bytes 4194304
  (14 shorter events, 0.2 us)
Async XLA Ops:
  0.6 86.8 %copy-start = (bf16[8192,128]{1,0:T(8,128)(2,1)S(1)}, bf16[8192,128]{1,0:T(8,128)(2,1)}, u32[]{:S(2)}) copy-start(bf16[8192,128]{1,0:T(8,128)(2,1)} %param.8) | copy-start | bytes 6291460
  4.4 16.8 %all-to-all-start = ((bf16[8,2,4096]{2,1,0:T(2,128)(2,1)}), bf16[8,2,4096]{2,1,0:T(2,128)(2,1)S(1)}, u32[]{:S(2)}, u32[]{:S(2)}) async-start(bf16[8,2,4096]{2,1,0:T(2,128)(2,1)} %reshape.61), calls=%async_computation | async-start | bytes 262144 | tf_op jit(solution)/shard_map/all_to_all | solution.py:22
  21.2 16.1 %all-to-all-start.5 = ((bf16[64,2,128]{2,1,0:T(2,128)(2,1)}), bf16[64,2,128]{2,1,0:T(2,128)(2,1)S(1)}, u32[]{:S(2)}, u32[]{:S(2)}) async-start(bf16[64,2,128]{2,1,0:T(2,128)(2,1)} %reshape.63), calls=%async_computation.5 | async-start | bytes 65536 | tf_op jit(solution)/shard_map/all_to_all | solution.py:40
  38.8 28.6 %all-to-all-start.1 = ((bf16[16,8,8192]{2,1,0:T(8,128)(2,1)}), bf16[16,8,8192]{2,1,0:T(8,128)(2,1)}, u32[]{:S(2)}, u32[]{:S(2)}) async-start(bf16[16,8,8192]{2,1,0:T(8,128)(2,1)} %broadcast_in_dim.43), calls=%async_computation.1 | async-start | bytes 4194304 | tf_op jit(solution)/shard_map/all_to_all | solution.py:22
  69.5 17.9 %copy-start.3 = (f32[128]{0:T(128)S(1)}, f32[128]{0:T(128)}, u32[]{:S(2)}) copy-start(f32[128]{0:T(128)} %param.9) | copy-start | bytes 1540
  81.9 10.6 %all-to-all-start.6 = ((bf16[4,64,256]{2,1,0:T(8,128)(2,1)}), bf16[4,64,256]{2,1,0:T(8,128)(2,1)S(1)}, u32[]{:S(2)}, u32[]{:S(2)}) async-start(bf16[4,64,256]{2,1,0:T(8,128)(2,1)} %stack.3), calls=%async_computation.6 | async-start | bytes 262144 | tf_op jit(solution)/shard_map/all_to_all | solution.py:13
  113.2 51.6 %all-to-all-start.4 = ((bf16[8,1024,256]{2,1,0:T(8,128)(2,1)}), bf16[8,1024,256]{2,1,0:T(8,128)(2,1)}, u32[]{:S(2)}, u32[]{:S(2)}) async-start(bf16[8,1024,256]{2,1,0:T(8,128)(2,1)} %broadcast_in_dim.48), calls=%async_computation.4 | async-start | bytes 8388608 | tf_op jit(solution)/shard_map/all_to_all | solution.py:22
  164.8 17.7 %copy-start.2 = (f32[256]{0:T(256)S(1)}, f32[256]{0:T(256)}, u32[]{:S(2)}) copy-start(f32[256]{0:T(256)} %param.11) | copy-start | bytes 3076
  164.8 17.7 %copy-start.1 = (bf16[8192,256]{1,0:T(8,128)(2,1)S(1)}, bf16[8192,256]{1,0:T(8,128)(2,1)}, u32[]{:S(2)}) copy-start(bf16[8192,256]{1,0:T(8,128)(2,1)} %param.10) | copy-start | bytes 12582916
  186.3 54.0 %all-to-all-start.7 = ((bf16[8,1024,256]{1,2,0:T(8,128)(2,1)}), bf16[8,1024,256]{1,2,0:T(8,128)(2,1)}, u32[]{:S(2)}, u32[]{:S(2)}) async-start(bf16[8,1024,256]{1,2,0:T(8,128)(2,1)} %bitcast.52), calls=%async_computation.7 | async-start | bytes 8388608 | tf_op jit(solution)/shard_map/all_to_all | solution.py:70
  241.6 13.8 %all-to-all-start.9 = ((f32[64,1,128]{2,1,0:T(1,128)}), f32[64,1,128]{2,1,0:T(1,128)S(1)}, u32[]{:S(2)}, u32[]{:S(2)}) async-start(f32[64,1,128]{2,1,0:T(1,128)} %broadcast_in_dim.49), calls=%async_computation.9 | async-start | bytes 65536 | tf_op jit(solution)/shard_map/all_to_all | solution.py:65
  255.4 19.1 %all-to-all-start.8 = ((bf16[8,128,256]{1,2,0:T(8,128)(2,1)}), bf16[8,128,256]{1,2,0:T(8,128)(2,1)S(1)}, u32[]{:S(2)}, u32[]{:S(2)}) async-start(bf16[8,128,256]{1,2,0:T(8,128)(2,1)} %copy_bitcast_fusion.1), calls=%async_computation.8 | async-start | bytes 1048576 | tf_op jit(solution)/shard_map/all_to_all | solution.py:78
